TPU v7x, 32 devices: a whole 2x2x4 slice. The times are simulated.
32 devices in a mesh: row: 4 (over y, x), col: 8 (over z, core).
Axes of the slice: x: 2, y: 2, z: 4, core: 2. Of those that a mesh axis runs over, the one named last changes fastest.
Arguments:
- features: bfloat16 [16384, 256], P(('col', 'row')), may hold values from -6 to 6
- weight: bfloat16 [256, 256], replicated, may hold values from -0.375 to 0.375
- cotangent: bfloat16 [16384, 256], P(('row', 'col')), may hold values from -6 to 6
- block_index: int32 [4, 8, 32], P('row', 'col'), may hold values from 0 to 511, as said below
- block_count: int32 [4, 8], P('row', 'col'), may hold values from 1 to 32, as said below
- block_values: bfloat16 [4, 8, 32, 128, 128], P('row', 'col'), may hold values from -0.25 to 0.25
Outputs:
- hidden_out: bfloat16 [16384, 256], P(('row', 'col'))
- input_grad: bfloat16 [16384, 256], P(('col', 'row'))
- weight_grad: float32 [256, 256], replicated
Inputs may be any that keep to these rules, and one draw needn't show every extreme that they name: `block_index`: the 32 entries of one tile are distinct; slots at or after the tile's count hold blocks that are not used. `block_count`: at least one tile holds exactly 32 blocks.
All inputs are finite; a program needn't handle non-finite values.
Results may differ from a plain program's by a relative error of at most 0.015.
Values may be sent and summed in bfloat16 or wider, within the bound.
No kernel may reach another device: no remote copies, remote signals or barrier semaphores. Data moves between devices by JAX's collectives and lax.ppermute only.
A program may use at most 64 MiB of HBM per device.

v0:
```python
import math
import jax
import jax.numpy as jnp
from jax import lax
from jax.sharding import PartitionSpec as P

GROUP = 32


def forward_tile(blocks_in, values, index, count, rows_out):
    ncols = blocks_in.shape[0]
    size = blocks_in.shape[1]
    width = blocks_in.shape[2]
    lanes = jnp.arange(GROUP, dtype=jnp.int32)
    targets = jnp.arange(rows_out, dtype=jnp.int32)

    def forward_advance(group_id, totals):
        start = (group_id * GROUP).astype(jnp.int32)
        live = start + lanes < count
        picked = jnp.take(blocks_in, index % ncols, axis=0)
        product = jnp.einsum("gij,gjd->gid", values, picked, preferred_element_type=jnp.float32)
        selector = ((index // ncols)[None, :] == targets[:, None]) & live[None, :]
        return totals + jnp.einsum(
            "rg,gid->rid", selector.astype(jnp.float32), product, precision=lax.Precision.HIGHEST
        )

    zeros = jnp.zeros((rows_out, size, width), jnp.float32)
    groups = (count + GROUP - 1) // GROUP
    return lax.fori_loop(jnp.int32(0), groups, forward_advance, zeros)


def backward_tile(blocks_grad, values, index, count, cols_out):
    size = blocks_grad.shape[1]
    width = blocks_grad.shape[2]
    lanes = jnp.arange(GROUP, dtype=jnp.int32)
    targets = jnp.arange(cols_out, dtype=jnp.int32)

    def backward_advance(group_id, totals):
        start = (group_id * GROUP).astype(jnp.int32)
        live = start + lanes < count
        picked = jnp.take(blocks_grad, index // cols_out, axis=0)
        product = jnp.einsum("gij,gid->gjd", values, picked, preferred_element_type=jnp.float32)
        selector = ((index % cols_out)[None, :] == targets[:, None]) & live[None, :]
        return totals + jnp.einsum(
            "cg,gjd->cjd", selector.astype(jnp.float32), product, precision=lax.Precision.HIGHEST
        )

    zeros = jnp.zeros((cols_out, size, width), jnp.float32)
    groups = (count + GROUP - 1) // GROUP
    return lax.fori_loop(jnp.int32(0), groups, backward_advance, zeros)


def body(features, weight, cotangent, block_index, block_count, block_values):
    row_total = lax.axis_size("row")
    col_total = lax.axis_size("col")
    rows = features.shape[0]
    width = features.shape[1]
    size = block_values.shape[-1]
    block_rows = rows * col_total // size
    block_cols = rows * row_total // size
    index = block_index[0, 0]
    count = block_count[0, 0]
    values = block_values[0, 0]
    gathered = lax.all_gather(features, "row", axis=0, tiled=True)
    projected = jnp.dot(gathered, weight, preferred_element_type=jnp.float32).astype(jnp.bfloat16)
    partial_out = forward_tile(
        projected.reshape(block_cols, size, width), values, index, count, block_rows
    )
    summed_out = lax.psum_scatter(
        partial_out.reshape(block_rows * size, width).astype(jnp.bfloat16),
        "col",
        scatter_dimension=0,
        tiled=True,
    )
    grad_rows = lax.all_gather(cotangent, "col", axis=0, tiled=True)
    partial_back = backward_tile(
        grad_rows.reshape(block_rows, size, width), values, index, count, block_cols
    )
    partial_back = partial_back.reshape(block_cols * size, width)
    grad_sum = lax.psum_scatter(
        partial_back.astype(jnp.bfloat16), "row", scatter_dimension=0, tiled=True
    ).astype(jnp.float32)
    input_grad = jnp.dot(
        grad_sum, weight.astype(jnp.float32).T, precision=lax.Precision.HIGHEST
    ).astype(jnp.bfloat16)
    term = jnp.einsum(
        "nd,ne->de", gathered, partial_back.astype(jnp.bfloat16), preferred_element_type=jnp.float32
    )
    total = lax.psum(term, ("row", "col"))
    nodes = rows * row_total * col_total
    weight_grad = total / math.sqrt(nodes)
    return (summed_out, input_grad, weight_grad)


def solution(mesh):
    in_specs = (
        P(("col", "row"), None),
        P(),
        P(("row", "col"), None),
        P("row", "col", None),
        P("row", "col"),
        P("row", "col", None, None, None),
    )
    out_specs = (P(("row", "col"), None), P(("col", "row"), None), P())
    return jax.shard_map(body, mesh=mesh, in_specs=in_specs, out_specs=out_specs, check_vma=False)
```

profile of v0, /device:TPU:0, one launch (start us, length us, event | category | flops | bytes accessed | tf_op | source)
XLA Modules:
  0.0 277.0 jit_solution(4447913578105518089)
XLA Ops:
  7.2 0.7 all-gather.5.cloned.1.call-update
  8.0 0.7 all-gather.3.cloned.1.call-update
  9.4 0.7 fusion.42
  10.0 0.7 bitcast_sign_fusion.1
  10.7 0.7 negate_bitcast_fusion
  11.4 30.1 %all-gather.5.cloned.1.call-done = bf16[4096,256]{1,0:T(8,128)(2,1)} async-done(((bf16[512,256]{1,0:T(8,128)(2,1)}), bf16[4096,256]{1,0:T(8,128)(2,1)}) %all-gather.5.cloned.1.call-update) | async-done | bytes 2097168 | tf_op jit(solution)/shard_map/all_gather | solution.py:75
  41.5 3.6 %gather_fusion.1 = bf16[32,128,256]{2,1,0:T(8,128)(2,1)} fusion(bf16[32,128,256]{2,1,0:T(8,128)(2,1)} %bitcast.94, s32[1024]{0:T(1024)S(1)} %pad_clamp_fusion.1), kind=kCustom, calls=%fused_computation.1 | custom fusion | bytes 4194432 | tf_op jit(solution)/shard_map/while/body/jit(_take)/gather | solution.py:41
  45.4 0.4 copy-done.3
  45.8 15.6 %while.34 = (s32[]{:T(128)}, f32[16,128,256]{2,0,1:T(8,128)S(1)}, s32[]{:T(128)}, s32[32]{0:T(128)S(1)}, s32[32]{0:T(128)S(1)}, /*index=5*/s32[]{:T(128)}, s32[3...) while((s32[]{:T(128)}, f32[16,128,256]{2,0,1:T(8,128)S(1)}, ...), condition=%wide.region_4.5_spmd.clone, body=%wide.region_3.4_spmd.clone.sunk | while | flops 471336928 | bytes 24118400 | solution.py:50
  45.8 0.7 compare_and_fusion.4
  46.5 4.6 %fusion.69 = f32[32,256,128]{2,1,0:T(8,128)} fusion(bf16[32,128,128]{2,1,0:T(8,128)(2,1)} %get-tuple-element.889, bf16[32,128,256]{2,1,0:T(8,128)(2,1)} %get-tuple-element.888, pred[32]{0:T(512)(128)(4,1)S(1)} %get-tuple-element.805), kind=kOutput, calls=%fused_computation.7.clone.1 | convolution fusion | flops 269484032 | bytes 7340064 | tf_op jit(solution)/shard_map/while/body/gij,gid->gjd/dot_general | solution.py:42
  51.1 5.5 %copy.20 = f32[32,256,128]{1,0,2:T(8,128)} copy(f32[32,256,128]{2,1,0:T(8,128)} %fusion.69) | data formatting | bytes 8388608 | tf_op jit(solution)/shard_map/while/body/gij,gid->gjd/dot_general | solution.py:42
  56.6 4.8 %fusion.70 = f32[16,128,256]{2,0,1:T(8,128)S(1)} fusion(f32[16,128,256]{2,0,1:T(8,128)S(1)} %get-tuple-element.871, f32[32,256,128]{1,0,2:T(8,128)} %copy.20, s32[32]{0:T(128)S(1)} %and_select_fusion.6, pred[32]{0:T(512)(128)(4,1)S(1)} %get-tuple-element.806), kind=kOutput, calls=%fused_computation.10.clone.1 | convolution fusion | flops 201851904 | bytes 8388768 | tf_op jit(solution)/shard_map/while/body/cg,gjd->cjd/dot_general | solution.py:44
  61.4 1.1 copy.17
  62.6 6.7 %all-gather.3.cloned.1.call-done = bf16[2048,256]{1,0:T(8,128)(2,1)} async-done(((bf16[512,256]{1,0:T(8,128)(2,1)}), bf16[2048,256]{1,0:T(8,128)(2,1)}) %all-gather.3.cloned.1.call-update) | async-done | bytes 1048592 | tf_op jit(solution)/shard_map/all_gather | solution.py:64
  69.3 2.5 convolution_bitcast_fusion
  71.9 0.4 convolution_convert_fusion
  72.4 2.5 broadcast_in_dim.62
  74.9 18.6 %while.35 = (s32[]{:T(128)}, f32[32,128,256]{2,0,1:T(8,128)}, s32[]{:T(128)}, s32[1,32]{1,0:T(1,128)S(1)}, s32[32]{0:T(128)S(1)}, /*index=5*/s32[1,32]{1,0:T(1,1...) while((s32[]{:T(128)}, f32[32,128,256]{2,0,1:T(8,128)}, ...), condition=%wide.region_1.2_spmd.clone.clone, body=%wide.region_0.1_spmd.clone.clone.sunk | while | flops 673190272 | bytes 32511760 | solution.py:29
  74.9 0.7 compare_and_fusion.5
  75.6 0.7 gather_fusion
  76.3 4.0 %fusion.76 = f32[32,256,128]{2,1,0:T(8,128)} fusion(bf16[32,128,128]{2,1,0:T(8,128)(2,1)} %get-tuple-element.856, bf16[32,128,256]{2,1,0:T(8,128)(2,1)S(1)} %gather_fusion, pred[32]{0:T(512)(128)(4,1)S(1)} %get-tuple-element.818), kind=kOutput, calls=%fused_computation.30.clone.1 | convolution fusion | flops 269484032 | bytes 7340064 | tf_op jit(solution)/shard_map/while/body/gij,gjd->gid/dot_general | solution.py:21
  80.3 5.5 %copy.21 = f32[32,256,128]{1,0,2:T(8,128)} copy(f32[32,256,128]{2,1,0:T(8,128)} %fusion.76) | data formatting | bytes 8388608 | tf_op jit(solution)/shard_map/while/body/gij,gjd->gid/dot_general | solution.py:21
  85.8 7.7 %fusion.78 = f32[32,128,256]{2,0,1:T(8,128)} fusion(f32[32,128,256]{2,0,1:T(8,128)} %get-tuple-element.834, f32[32,256,128]{1,0,2:T(8,128)} %copy.21, s32[32]{0:T(128)S(1)} %fusion.77, pred[32]{0:T(512)(128)(4,1)S(1)} %get-tuple-element.819), kind=kOutput, calls=%fused_computation.29.clone.1 | convolution fusion | flops 403703808 | bytes 12583072 | tf_op jit(solution)/shard_map/while/body/rg,gid->rid/dot_general | solution.py:23
  93.5 2.5 convert_element_type.25
  96.0 2.5 copy.11
  98.6 103.3 %all-reduce.2.cloned.1.call-done = f32[256,256]{0,1:T(8,128)} async-done(((f32[256,256]{0,1:T(8,128)}), f32[256,256]{0,1:T(8,128)}) %all-reduce.2.cloned.1.call-update) | async-done | bytes 262160 | tf_op jit(solution)/shard_map/psum | solution.py:89
  201.9 1.0 broadcast_multiply_fusion
  202.9 0.8 copy.13
  203.7 27.9 %reduce-scatter.5.cloned.1.call-done = bf16[512,256]{1,0:T(8,128)(2,1)} async-done(((bf16[2048,256]{1,0:T(8,128)(2,1)}), bf16[512,256]{1,0:T(8,128)(2,1)}) %reduce-scatter.5.cloned.1.call-update) | async-done | bytes 262160 | tf_op jit(solution)/shard_map/reduce_scatter | solution.py:80
  231.7 1.9 convolution_convert_fusion.1
  233.6 36.9 %reduce-scatter.3.cloned.1.call-done = bf16[512,256]{1,0:T(8,128)(2,1)} async-done(((bf16[4096,256]{1,0:T(8,128)(2,1)}), bf16[512,256]{1,0:T(8,128)(2,1)}) %reduce-scatter.3.cloned.1.call-update) | async-done | bytes 262160 | tf_op jit(solution)/shard_map/reduce_scatter | solution.py:69
  (21 shorter events, 0.6 us)
Async XLA Ops:
  7.2 64.7 %copy-start = (bf16[256,256]{1,0:T(8,128)(2,1)S(1)}, bf16[256,256]{1,0:T(8,128)(2,1)}, u32[]{:S(2)}) copy-start(bf16[256,256]{1,0:T(8,128)(2,1)} %param.11) | copy-start | bytes 393220
  7.2 34.3 %all-gather.5.cloned.1.call-start = ((), (), s32[]{:S(2)}) async-start(), calls=%async_computation.4 | async-start | bytes 2359296 | tf_op jit(solution)/shard_map/all_gather | solution.py:75
  7.9 61.3 %all-gather.3.cloned.1.call-start = ((), (), s32[]{:S(2)}) async-start(), calls=%async_computation.2 | async-start | bytes 1310720 | tf_op jit(solution)/shard_map/all_gather | solution.py:64
  8.7 193.3 %all-reduce.2.cloned.1.call-start = ((), (), s32[]{:S(2)}) async-start(), calls=%async_computation.6 | async-start | bytes 524288 | tf_op jit(solution)/shard_map/psum | solution.py:89
  45.1 0.7 copy-start.3
  62.6 9.2 %copy-start.1 = (bf16[16,128,256]{2,1,0:T(8,128)(2,1)}, bf16[16,128,256]{2,1,0:T(8,128)(2,1)S(1)}, u32[]{:S(2)}) copy-start(bf16[16,128,256]{2,1,0:T(8,128)(2,1)S(1)} %copy.17) | copy-start | bytes 3145732
  69.3 2.6 copy-start.2
  71.8 159.9 %reduce-scatter.5.cloned.1.call-start = ((), (), s32[]{:S(2)}) async-start(), calls=%async_computation.5 | async-start | bytes 1310720 | tf_op jit(solution)/shard_map/reduce_scatter | solution.py:80
  72.4 198.1 %reduce-scatter.3.cloned.1.call-start = ((), (), s32[]{:S(2)}) async-start(), calls=%async_computation.3 | async-start | bytes 2359296 | tf_op jit(solution)/shard_map/reduce_scatter | solution.py:69
Sparse Core Ops, SparseCore 0:
  9.6 31.8 all-gather.4
  43.3 25.8 all-gather.2
  75.3 126.5 all-reduce.1
  204.7 26.9 reduce-scatter.4
  234.4 36.0 reduce-scatter.2
where the time goes:
time: 278 us; the launch traced here: 277 us
  waiting for transfers between devices  206 us (74%)
  matrix products  26 us (9%)
  local copies, waits for them, and re-layouts  22.9 us (8%)
  between operations  14.5 us (5%)
  other arithmetic  6.83 us (2%)
    psum x1, waiting for transfers between devices, body(): total = lax.psum(term, ('row', 'col'))  103 us
    reduce_scatter x1, waiting for transfers between devices, body(): lax.psum_scatter(partial_out.reshape(block_rows * size, width).astype(jnp...  36.9 us
    all_gather x1, waiting for transfers between devices, body(): grad_rows = lax.all_gather(cotangent, 'col', axis=0, tiled=True)  30.1 us
    reduce_scatter x1, waiting for transfers between devices, body(): lax.psum_scatter(partial_back.astype(jnp.bfloat16), 'row', scatter_dimens...  27.9 us
    dot_general x1, matrix products, forward_advance(): jnp.einsum('rg,gid->rid', selector.astype(jnp.float32), product, precisio...  7.68 us
    all_gather x1, waiting for transfers between devices, body(): gathered = lax.all_gather(features, 'row', axis=0, tiled=True)  6.68 us
  transfers between devices with their start and end apart: 5, of which 5 were waited for; matrix products, arithmetic and copies ran while one was open for 19% of the time, Pallas kernels for 0%

commit v1 on v0

--- a/solution.py
+++ b/solution.py
@@ -5,6 +5,29 @@
 from jax.sharding import PartitionSpec as P
 
 GROUP = 32
+
+
+def joined_along(blocks, dim):
+    shape = list(blocks.shape[1:])
+    shape[dim] *= blocks.shape[0]
+    return jnp.moveaxis(blocks, 0, dim).reshape(shape)
+
+
+def collected_by_bits(value, axis):
+    count, mine = (lax.axis_size(axis), lax.axis_index(axis))
+    blocks, distance = (value[None], 1)
+    while distance < count:
+        received = lax.ppermute(blocks, axis, [(i, i ^ distance) for i in range(count)])
+        low = mine & distance == 0
+        blocks = jnp.concatenate(
+            [jnp.where(low, blocks, received), jnp.where(low, received, blocks)]
+        )
+        distance *= 2
+    return blocks
+
+
+def collect(shard, axis, dim):
+    return joined_along(collected_by_bits(shard, axis), dim)
 
 
 def forward_tile(blocks_in, values, index, count, rows_out):
@@ -72,7 +95,7 @@
         scatter_dimension=0,
         tiled=True,
     )
-    grad_rows = lax.all_gather(cotangent, "col", axis=0, tiled=True)
+    grad_rows = collect(cotangent, "col", 0)
     partial_back = backward_tile(
         grad_rows.reshape(block_rows, size, width), values, index, count, block_cols
     )

time: 278 us -> 299 us (1.076)
  waiting for transfers between devices: 206 us -> 224 us
  starting transfers between devices: 0.2 us -> 6.54 us
    ppermute x0 -> x3, waiting for transfers between devices: none -> 58 us  [collected_by_bits(): lax.ppermute(blocks, axis, [(i, i ^ distance) for i in range(count)])]
    all_gather x1 -> x0, waiting for transfers between devices: 30.1 us -> none  [body(): grad_rows = lax.all_gather(cotangent, 'col', axis=0, tiled=True)]
    all_gather x1, waiting for transfers between devices: 6.68 us -> 0.02 us  [body(): gathered = lax.all_gather(features, 'row', axis=0, tiled=True)]
    ppermute x0 -> x3, starting transfers between devices: none -> 6.37 us  [collected_by_bits(): lax.ppermute(blocks, axis, [(i, i ^ distance) for i in range(count)])]
  transfers between devices with their start and end apart: 5 -> 7, of which waited for: 5 -> 6; matrix products, arithmetic and copies ran while one was open for 19% -> 17% of each run, Pallas kernels for 0% -> 0%
where the time goes in v1:
time: 299 us
  waiting for transfers between devices  224 us (75%)
  matrix products  26.3 us (9%)
  local copies, waits for them, and re-layouts  21 us (7%)
  between operations  14.6 us (5%)
  starting transfers between devices  6.54 us (2%)
  other arithmetic  6.4 us (2%)
    psum x1, waiting for transfers between devices, body(): total = lax.psum(term, ('row', 'col'))  101 us
    ppermute x3, waiting for transfers between devices, collected_by_bits(): lax.ppermute(blocks, axis, [(i, i ^ distance) for i in range(count)])  58 us
    reduce_scatter x1, waiting for transfers between devices, body(): lax.psum_scatter(partial_out.reshape(block_rows * size, width).astype(jnp...  36.6 us
    reduce_scatter x1, waiting for transfers between devices, body(): lax.psum_scatter(partial_back.astype(jnp.bfloat16), 'row', scatter_dimens...  28.1 us
    dot_general x1, matrix products, forward_advance(): jnp.einsum('rg,gid->rid', selector.astype(jnp.float32), product, precisio...  7.69 us
    ppermute x3, starting transfers between devices, collected_by_bits(): lax.ppermute(blocks, axis, [(i, i ^ distance) for i in range(count)])  6.37 us
  transfers between devices with their start and end apart: 7, of which 6 were waited for; matrix products, arithmetic and copies ran while one was open for 17% of the time, Pallas kernels for 0%

profile of v1, /device:TPU:0, one launch (start us, length us, event | category | flops | bytes accessed | tf_op | source)
XLA Modules:
  0.0 298.7 jit_solution(5794929942287257078)
XLA Ops:
  7.2 0.6 collective-permute-start
  7.8 1.4 collective-permute-done
  9.2 1.0 broadcast_select_fusion.5
  10.2 3.0 %collective-permute-start.1 = (bf16[2,512,256]{2,1,0:T(8,128)(2,1)S(1)}, bf16[2,512,256]{2,1,0:T(8,128)(2,1)S(1)}, u32[]{:S(2)}, u32[]{:S(2)}) collective-permute-start(bf16[2,512,256]{2,1,0:T(8,128)(2,1)S(1)} %pad_maximum_fusion.2), channel_id=1, source_target_pairs={{0,2},{1,3},{2,0},{3,1},{4,6},{5,7},{6,4},{7,5},{8,10},{9,11},{10,... | collective-permute-start | bytes 1572872 | tf_op jit(solution)/shard_map/ppermute | solution.py:20
  13.2 12.2 %collective-permute-done.1 = bf16[2,512,256]{2,1,0:T(8,128)(2,1)S(1)} collective-permute-done((bf16[2,512,256]{2,1,0:T(8,128)(2,1)S(1)}, bf16[2,512,256]{2,1,0:T(8,128)(2,1)S(1)}, u32[]{:S(2)}, u32[]{:S(2)}) %collective-permute-start.1) | collective-permute-done | bytes 524320 | tf_op jit(solution)/shard_map/ppermute | solution.py:20
  25.6 2.8 collective-permute-start.2
  29.2 44.4 %collective-permute-done.2 = bf16[4,512,256]{2,1,0:T(8,128)(2,1)S(1)} collective-permute-done((bf16[4,512,256]{2,1,0:T(8,128)(2,1)S(1)}, bf16[4,512,256]{2,1,0:T(8,128)(2,1)S(1)}, u32[]{:S(2)}, u32[]{:S(2)}) %collective-permute-start.2) | collective-permute-done | bytes 1048608 | tf_op jit(solution)/shard_map/ppermute | solution.py:20
  74.0 2.1 gather_fusion.1
  76.1 0.2 broadcast_in_dim.66
  76.3 15.7 %while.34 = (s32[]{:T(128)}, f32[16,128,256]{2,0,1:T(8,128)S(1)}, s32[]{:T(128)}, s32[32]{0:T(128)S(1)}, s32[32]{0:T(128)S(1)}, /*index=5*/s32[]{:T(128)}, s32[3...) while((s32[]{:T(128)}, f32[16,128,256]{2,0,1:T(8,128)S(1)}, ...), condition=%wide.region_4.5_spmd.clone, body=%wide.region_3.4_spmd.clone.sunk | while | flops 471336928 | bytes 24118400 | solution.py:73
  76.3 0.7 compare_and_fusion.4
  77.0 4.6 %fusion.69 = f32[32,256,128]{2,1,0:T(8,128)} fusion(bf16[32,128,128]{2,1,0:T(8,128)(2,1)} %get-tuple-element.895, bf16[32,128,256]{2,1,0:T(8,128)(2,1)} %get-tuple-element.894, pred[32]{0:T(512)(128)(4,1)S(1)} %get-tuple-element.811), kind=kOutput, calls=%fused_computation.7.clone.1 | convolution fusion | flops 269484032 | bytes 7340064 | tf_op jit(solution)/shard_map/while/body/gij,gid->gjd/dot_general | solution.py:65
  81.6 5.5 %copy.20 = f32[32,256,128]{1,0,2:T(8,128)} copy(f32[32,256,128]{2,1,0:T(8,128)} %fusion.69) | data formatting | bytes 8388608 | tf_op jit(solution)/shard_map/while/body/gij,gid->gjd/dot_general | solution.py:65
  87.2 4.8 %fusion.70 = f32[16,128,256]{2,0,1:T(8,128)S(1)} fusion(f32[16,128,256]{2,0,1:T(8,128)S(1)} %get-tuple-element.877, f32[32,256,128]{1,0,2:T(8,128)} %copy.20, s32[32]{0:T(128)S(1)} %and_select_fusion.6, pred[32]{0:T(512)(128)(4,1)S(1)} %get-tuple-element.812), kind=kOutput, calls=%fused_computation.10.clone.1 | convolution fusion | flops 201851904 | bytes 8388768 | tf_op jit(solution)/shard_map/while/body/cg,gjd->cjd/dot_general | solution.py:67
  92.0 1.1 copy.17
  93.2 2.8 convolution_bitcast_fusion
  96.1 0.4 convolution_convert_fusion
  96.8 2.5 broadcast_in_dim.65
  99.3 18.6 %while.35 = (s32[]{:T(128)}, f32[32,128,256]{2,0,1:T(8,128)}, s32[]{:T(128)}, s32[1,32]{1,0:T(1,128)S(1)}, s32[32]{0:T(128)S(1)}, /*index=5*/s32[1,32]{1,0:T(1,1...) while((s32[]{:T(128)}, f32[32,128,256]{2,0,1:T(8,128)}, ...), condition=%wide.region_1.2_spmd.clone.clone, body=%wide.region_0.1_spmd.clone.clone.sunk | while | flops 673190272 | bytes 32511760 | solution.py:52
  99.3 0.7 compare_and_fusion.5
  100.0 0.7 gather_fusion
  100.7 4.0 %fusion.76 = f32[32,256,128]{2,1,0:T(8,128)} fusion(bf16[32,128,128]{2,1,0:T(8,128)(2,1)} %get-tuple-element.862, bf16[32,128,256]{2,1,0:T(8,128)(2,1)S(1)} %gather_fusion, pred[32]{0:T(512)(128)(4,1)S(1)} %get-tuple-element.824), kind=kOutput, calls=%fused_computation.30.clone.1 | convolution fusion | flops 269484032 | bytes 7340064 | tf_op jit(solution)/shard_map/while/body/gij,gjd->gid/dot_general | solution.py:44
  104.7 5.5 %copy.21 = f32[32,256,128]{1,0,2:T(8,128)} copy(f32[32,256,128]{2,1,0:T(8,128)} %fusion.76) | data formatting | bytes 8388608 | tf_op jit(solution)/shard_map/while/body/gij,gjd->gid/dot_general | solution.py:44
  110.2 7.7 %fusion.78 = f32[32,128,256]{2,0,1:T(8,128)} fusion(f32[32,128,256]{2,0,1:T(8,128)} %get-tuple-element.840, f32[32,256,128]{1,0,2:T(8,128)} %copy.21, s32[32]{0:T(128)S(1)} %fusion.77, pred[32]{0:T(512)(128)(4,1)S(1)} %get-tuple-element.825), kind=kOutput, calls=%fused_computation.29.clone.1 | convolution fusion | flops 403703808 | bytes 12583072 | tf_op jit(solution)/shard_map/while/body/rg,gid->rid/dot_general | solution.py:46
  117.9 2.5 convert_element_type.25
  120.4 2.5 copy.11
  123.0 100.7 %all-reduce.2.cloned.1.call-done = f32[256,256]{0,1:T(8,128)} async-done(((f32[256,256]{0,1:T(8,128)}), f32[256,256]{0,1:T(8,128)}) %all-reduce.2.cloned.1.call-update) | async-done | bytes 262160 | tf_op jit(solution)/shard_map/psum | solution.py:112
  223.7 1.0 broadcast_multiply_fusion
  224.7 0.8 copy.13
  225.5 28.1 %reduce-scatter.5.cloned.1.call-done = bf16[512,256]{1,0:T(8,128)(2,1)} async-done(((bf16[2048,256]{1,0:T(8,128)(2,1)}), bf16[512,256]{1,0:T(8,128)(2,1)}) %reduce-scatter.5.cloned.1.call-update) | async-done | bytes 262160 | tf_op jit(solution)/shard_map/reduce_scatter | solution.py:103
  253.6 1.9 convolution_convert_fusion.1
  255.5 36.6 %reduce-scatter.3.cloned.1.call-done = bf16[512,256]{1,0:T(8,128)(2,1)} async-done(((bf16[4096,256]{1,0:T(8,128)(2,1)}), bf16[512,256]{1,0:T(8,128)(2,1)}) %reduce-scatter.3.cloned.1.call-update) | async-done | bytes 262160 | tf_op jit(solution)/shard_map/reduce_scatter | solution.py:92
  (30 shorter events, 1.1 us)
Async XLA Ops:
  7.2 88.9 %copy-start = (bf16[256,256]{1,0:T(8,128)(2,1)S(1)}, bf16[256,256]{1,0:T(8,128)(2,1)}, u32[]{:S(2)}) copy-start(bf16[256,256]{1,0:T(8,128)(2,1)} %param.11) | copy-start | bytes 393220
  7.2 86.0 %all-gather.2.cloned.1.call-start = ((), (), s32[]{:S(2)}) async-start(), calls=%async_computation.2 | async-start | bytes 1310720 | tf_op jit(solution)/shard_map/all_gather | solution.py:87
  7.2 1.9 collective-permute-start
  10.2 15.2 %collective-permute-start.1 = (bf16[2,512,256]{2,1,0:T(8,128)(2,1)S(1)}, bf16[2,512,256]{2,1,0:T(8,128)(2,1)S(1)}, u32[]{:S(2)}, u32[]{:S(2)}) collective-permute-start(bf16[2,512,256]{2,1,0:T(8,128)(2,1)S(1)} %pad_maximum_fusion.2), channel_id=1, source_target_pairs={{0,2},{1,3},{2,0},{3,1},{4,6},{5,7},{6,4},{7,5},{8,10},{9,11},{10,... | collective-permute-start | bytes 1572872 | tf_op jit(solution)/shard_map/ppermute | solution.py:20
  13.2 16.0 %copy-start.3 = (s32[1,1,32]{2,1,0:T(1,128)S(1)}, s32[1,1,32]{2,1,0:T(1,128)}, u32[]{:S(2)}) copy-start(s32[1,1,32]{2,1,0:T(1,128)} %param.13) | copy-start | bytes 388
  25.6 48.1 %collective-permute-start.2 = (bf16[4,512,256]{2,1,0:T(8,128)(2,1)S(1)}, bf16[4,512,256]{2,1,0:T(8,128)(2,1)S(1)}, u32[]{:S(2)}, u32[]{:S(2)}) collective-permute-start(bf16[4,512,256]{2,1,0:T(8,128)(2,1)S(1)} %pad_maximum_fusion.1), channel_id=1, source_target_pairs={{0,4},{1,5},{2,6},{3,7},{4,0},{5,1},{6,2},{7,3},{8,12},{9,13},{10,... | collective-permute-start | bytes 3145736 | tf_op jit(solution)/shard_map/ppermute | solution.py:20
  28.5 195.2 %all-reduce.2.cloned.1.call-start = ((), (), s32[]{:S(2)}) async-start(), calls=%async_computation.5 | async-start | bytes 524288 | tf_op jit(solution)/shard_map/psum | solution.py:112
  93.1 2.9 copy-start.1
  93.2 2.9 copy-start.2
  96.0 157.6 %reduce-scatter.5.cloned.1.call-start = ((), (), s32[]{:S(2)}) async-start(), calls=%async_computation.4 | async-start | bytes 1310720 | tf_op jit(solution)/shard_map/reduce_scatter | solution.py:103
  96.7 195.4 %reduce-scatter.3.cloned.1.call-start = ((), (), s32[]{:S(2)}) async-start(), calls=%async_computation.3 | async-start | bytes 2359296 | tf_op jit(solution)/shard_map/reduce_scatter | solution.py:92
Sparse Core Ops, SparseCore 0:
  28.6 25.7 all-gather.1
  96.1 127.5 all-reduce.1
  226.6 26.9 reduce-scatter.4
  256.3 35.7 reduce-scatter.2
